TPU v7x, 32 devices: a whole 2x2x4 slice. The times are simulated.
32 devices in a mesh: dp: 16 (over z, y, core), seq: 2 (over x).
Axes of the slice: x: 2, y: 2, z: 4, core: 2. Of those that a mesh axis runs over, the one named last changes fastest.
Arguments:
- pre_act: bfloat16 [16, 512, 768], P('dp', 'seq'), may hold values from -6 to 6
- trunk_grad: bfloat16 [16, 256, 768], P('dp', None, 'seq'), may hold values from -6 to 6
- conv_weight: bfloat16 [5, 768, 768], P(None, 'dp'), may hold values from -0.09375 to 0.09375
- pair_weight: bfloat16 [768, 768], replicated, may hold values from -0.21875 to 0.21875
- donor_slots: int32 [16, 2, 2, 128], P('dp', 'seq'), may hold values from 0 to 255
- accept_slots: int32 [16, 2, 2, 128], P('dp', 'seq'), may hold values from 0 to 255
- junction_grad: float32 [16, 2, 2, 128], P('dp', 'seq'), may hold values from -6 to 6
- pair_counts: int32 [16, 2, 2], P('dp'), may hold values from 0 to 128, as said below
Outputs:
- input_grad: bfloat16 [16, 512, 768], P('dp', 'seq')
- pair_grad: float32 [768, 768], replicated
Inputs may be any that keep to these rules, and one draw needn't show every extreme that they name: pair_counts is at most 128; in every sample some acceptor slab has 128 live slots from every donor slab.
All inputs are finite; a program needn't handle non-finite values.
Results may differ from a plain program's by a relative error of at most 0.0061.
Values may be sent and summed in bfloat16 or wider, within the bound.
A program may use at most 64 MiB of HBM per device.

v0:
```python
import math
import jax
import jax.numpy as jnp
from jax import lax
from jax.sharding import PartitionSpec as P


def with_halo(x, sides, width):
    for axis, dim in sides:
        size, length = (lax.axis_size(axis), x.shape[dim])
        up = [(i, (i + 1) % size) for i in range(size - 1)]
        down = [(j, i) for i, j in up]
        last = lax.slice_in_dim(x, length - width, length, axis=dim)
        first = lax.slice_in_dim(x, 0, width, axis=dim)
        before = lax.ppermute(last, axis, up)
        after = lax.ppermute(first, axis, down)
        x = jnp.concatenate([before, x, after], axis=dim)
    return x


def gelu_parts(values):
    normal_cdf = 0.5 * (1.0 + jax.scipy.special.erf(values / math.sqrt(2.0)))
    density = jnp.exp(-0.5 * values * values) / math.sqrt(2.0 * math.pi)
    return (values * normal_cdf, normal_cdf + values * density)


def per_device(
    pre_act,
    trunk_grad,
    conv_weight,
    pair_weight,
    donor_slots,
    accept_slots,
    junction_grad,
    pair_counts,
):
    seq_count = lax.axis_size("seq")
    my_slab = lax.axis_index("seq")
    slab_len = pre_act.shape[1]
    channels = pre_act.shape[2]
    slot_count = donor_slots.shape[3]
    kernel = conv_weight.shape[0]
    half = kernel // 2
    act_f, slope = gelu_parts(pre_act[0].astype(jnp.float32))
    act = act_f.astype(jnp.bfloat16)
    arrived = lax.all_to_all(trunk_grad, "seq", split_axis=1, concat_axis=2, tiled=True)
    pooled = jnp.repeat(arrived[0].astype(jnp.float32) * 0.5, 2, axis=0)
    send_index = donor_slots[0, 0].reshape(-1)
    outgoing = act[send_index].reshape(seq_count, slot_count, channels)
    incoming = lax.all_to_all(outgoing, "seq", split_axis=0, concat_axis=0, tiled=True)
    donor_rows = incoming.reshape(-1, channels)
    accept_index = accept_slots[0, 0].reshape(-1)
    counts_in = lax.dynamic_index_in_dim(pair_counts[0], my_slab, axis=1, keepdims=False)
    live = jnp.arange(slot_count, dtype=jnp.int32)[None, :] < counts_in[:, None]
    slot_w = jnp.where(live, junction_grad[0, 0], 0.0).reshape(-1)
    accept_rows = act[accept_index]
    weighted = (slot_w[:, None] * accept_rows.astype(jnp.float32)).astype(jnp.bfloat16)
    accept_term = (
        jnp.dot(donor_rows, pair_weight, preferred_element_type=jnp.float32) * slot_w[:, None]
    )
    donor_term = lax.dot_general(
        weighted, pair_weight, (((1,), (1,)), ((), ())), preferred_element_type=jnp.float32
    ).astype(jnp.bfloat16)
    pair_part = lax.dot_general(
        donor_rows, weighted, (((0,), (0,)), ((), ())), preferred_element_type=jnp.float32
    )
    returned = lax.all_to_all(
        donor_term.reshape(seq_count, slot_count, channels),
        "seq",
        split_axis=0,
        concat_axis=0,
        tiled=True,
    )
    act_grad = (
        pooled.at[accept_index]
        .add(accept_term)
        .at[send_index]
        .add(returned.reshape(-1, channels).astype(jnp.float32))
    )
    conv_grad = (act_grad * slope).astype(jnp.bfloat16)
    padded = with_halo(conv_grad[None], (("seq", 1),), half)[0]
    piece = lax.all_gather(conv_weight, "dp", axis=1, tiled=True)
    total = jnp.zeros((slab_len, piece.shape[1]), jnp.float32)
    for tap in range(kernel):
        window = padded[2 * half - tap : 2 * half - tap + slab_len]
        total = total + lax.dot_general(
            window, piece[tap], (((1,), (1,)), ((), ())), preferred_element_type=jnp.float32
        )
    input_grad = total.astype(jnp.bfloat16)
    pair_sum = lax.psum(pair_part, ("dp", "seq"))
    scale = 1.0 / math.sqrt(lax.axis_size("dp") * seq_count * seq_count * slot_count)
    return (input_grad[None], pair_sum * scale)


def solution(mesh):
    in_specs = (
        P("dp", "seq", None),
        P("dp", None, "seq"),
        P(None, "dp", None),
        P(),
        P("dp", "seq", None, None),
        P("dp", "seq", None, None),
        P("dp", "seq", None, None),
        P("dp", None, None),
    )
    out_specs = (P("dp", "seq", None), P())
    return jax.shard_map(
        per_device, mesh=mesh, in_specs=in_specs, out_specs=out_specs, check_vma=False
    )
```

profile of v0, /device:TPU:0, one launch (start us, length us, event | category | flops | bytes accessed | tf_op | source)
XLA Modules:
  0.0 200.0 jit_solution(1862598864620470224)
XLA Ops:
  8.0 0.0 copy-start
  8.0 1.3 fusion.6
  9.3 0.0 copy-start.4
  9.3 0.7 compare_select_fusion
  10.0 1.9 gather_fusion
  11.9 0.0 copy-start.5
  11.9 0.0 copy-start.6
  11.9 4.3 %all-to-all-start.1 = ((bf16[2,128,768]{2,1,0:T(8,128)(2,1)}), bf16[2,128,768]{2,1,0:T(8,128)(2,1)S(1)}, u32[]{:S(2)}, u32[]{:S(2)}) async-start(bf16[2,128,768]{2,1,0:T(8,128)(2,1)} %bitcast.9), calls=%async_computation.1 | async-start | bytes 786432 | tf_op jit(solution)/shard_map/all_to_all | solution.py:50
  16.3 0.0 all-reduce.2.cloned.1.call-start
  16.3 0.0 copy-done.4
  16.3 1.2 gather_fusion.1
  17.5 0.0 copy-done.5
  17.5 0.2 dynamic-slice_reduce_fusion
  17.7 0.0 copy-done.6
  17.7 0.1 bitcast_select_fusion
  17.8 5.8 %all-to-all-done.1 = bf16[2,128,768]{2,1,0:T(8,128)(2,1)S(1)} async-done(((bf16[2,128,768]{2,1,0:T(8,128)(2,1)}), bf16[2,128,768]{2,1,0:T(8,128)(2,1)S(1)}, u32[]{:S(2)}, u32[]{:S(2)}) %all-to-all-start.1) | async-done | bytes 393248 | tf_op jit(solution)/shard_map/all_to_all | solution.py:50
  23.6 0.0 copy-start.3
  23.6 2.0 fusion.26
  25.6 0.0 all-reduce.2.cloned.1.call-update
  25.6 0.0 all-gather.2.cloned.1.call-start
  25.6 0.5 all-gather.2.cloned.1.call-update
  26.2 0.0 copy-done.3
  26.2 0.3 copy.19
  26.5 0.5 broadcast.65
  27.0 1.8 reduce.2
  28.8 0.7 reshape.152
  29.5 3.4 %all-to-all-start = ((bf16[2,2,24576]{2,1,0:T(2,128)(2,1)}), bf16[2,2,24576]{2,1,0:T(2,128)(2,1)S(1)}, u32[]{:S(2)}, u32[]{:S(2)}) async-start(bf16[2,2,24576]{2,1,0:T(2,128)(2,1)} %reshape.152), calls=%async_computation | async-start | bytes 393216 | tf_op jit(solution)/shard_map/all_to_all | solution.py:46
  33.0 0.0 copy-done
  33.0 1.3 convolution_convert_fusion
  34.3 4.3 %all-to-all-done = bf16[2,2,24576]{2,1,0:T(2,128)(2,1)S(1)} async-done(((bf16[2,2,24576]{2,1,0:T(2,128)(2,1)}), bf16[2,2,24576]{2,1,0:T(2,128)(2,1)S(1)}, u32[]{:S(2)}, u32[]{:S(2)}) %all-to-all-start) | async-done | bytes 196640 | tf_op jit(solution)/shard_map/all_to_all | solution.py:46
  38.6 4.2 %all-to-all-start.2 = ((bf16[2,128,768]{2,1,0:T(8,128)(2,1)}), bf16[2,128,768]{2,1,0:T(8,128)(2,1)}, u32[]{:S(2)}, u32[]{:S(2)}) async-start(bf16[2,128,768]{2,1,0:T(8,128)(2,1)} %bitcast.13), calls=%async_computation.2 | async-start | bytes 786432 | tf_op jit(solution)/shard_map/all_to_all | solution.py:67
  42.8 0.2 reshape.153
  43.0 0.2 copy.15
  43.2 0.2 copy.16
  43.4 0.3 broadcast_in_dim.10
  43.7 0.5 reshape.111
  44.2 0.5 convolution_multiply_fusion
  44.7 0.0 copy-start.1
  44.7 2.5 %scatter_fusion = f32[256,768]{1,0:T(8,128)S(1)} fusion(f32[256,768]{1,0:T(8,128)S(1)} %reshape.111, s32[256]{0:T(256)S(1)} %bitcast.77, f32[256,768]{1,0:T(8,128)S(1)} %convolution_multiply_fusion), kind=kCustom, calls=%fused_computation.2 | custom fusion | flops 196608 | bytes 2360320 | tf_op jit(solution)/shard_map/scatter-add | solution.py:76
  47.3 2.6 %all-to-all-done.2 = bf16[2,128,768]{2,1,0:T(8,128)(2,1)} async-done(((bf16[2,128,768]{2,1,0:T(8,128)(2,1)}), bf16[2,128,768]{2,1,0:T(8,128)(2,1)}, u32[]{:S(2)}, u32[]{:S(2)}) %all-to-all-start.2) | async-done | bytes 393248 | tf_op jit(solution)/shard_map/all_to_all | solution.py:67
  49.9 3.0 %scatter_custom_fusion.1 = f32[256,768]{1,0:T(8,128)S(1)} fusion(f32[256,768]{1,0:T(8,128)S(1)} %scatter_fusion, s32[256]{0:T(256)S(1)} %bitcast.79, bf16[256,768]{1,0:T(8,128)(2,1)} %bitcast.27), kind=kCustom, calls=%fused_computation.33 | custom fusion | flops 393216 | bytes 1179648 | tf_op jit(solution)/shard_map/scatter-add | solution.py:78
  52.9 0.0 copy-done.1
  52.9 0.4 fusion.11
  53.3 1.3 collective-permute-start
  54.6 4.7 %collective-permute-start.1 = (bf16[1,2,768]{2,1,0:T(2,128)(2,1)S(1)}, bf16[1,2,768]{2,1,0:T(2,128)(2,1)S(1)}, u32[]{:S(2)}, u32[]{:S(2)}) collective-permute-start(bf16[1,2,768]{2,1,0:T(2,128)(2,1)S(1)} %get-tuple-element.2), channel_id=1, source_target_pairs={{0,1},{2,3},{4,5},{6,7},{8,9},{10,11},{12,13},{14,15},{16,17},{18,... | collective-permute-start | bytes 9224 | tf_op jit(solution)/shard_map/ppermute | solution.py:15
  59.3 123.8 %all-reduce.2.cloned.1.call-done = f32[768,768]{1,0:T(8,128)} async-done(((f32[768,768]{1,0:T(8,128)}), f32[768,768]{1,0:T(8,128)}) %all-reduce.2.cloned.1.call-update) | async-done | bytes 2359312 | tf_op jit(solution)/shard_map/psum | solution.py:90
  183.1 3.3 %broadcast_multiply_fusion = f32[768,768]{1,0:T(8,128)} fusion(f32[768,768]{1,0:T(8,128)} %all-reduce.2.cloned.1.call-done), kind=kLoop, calls=%fused_computation.23 | loop fusion | flops 589824 | bytes 4718592 | tf_op jit(solution)/shard_map/mul | solution.py:92
  186.4 0.0 collective-permute-done
  186.4 0.0 all-gather.2.cloned.1.call-done
  186.4 0.0 copy-start.2
  186.4 1.9 fusion.2
  188.3 1.9 convolution_add_fusion.3
  190.2 0.0 copy-done.2
  190.3 0.5 convolution_add_fusion.2
  190.8 0.0 collective-permute-done.1
  190.8 0.5 convolution_add_fusion.1
  191.3 1.3 fusion.1
  (5 shorter events, 0.1 us)
Async XLA Ops:
  8.0 25.0 %copy-start = (bf16[768,768]{1,0:T(8,128)(2,1)S(1)}, bf16[768,768]{1,0:T(8,128)(2,1)}, u32[]{:S(2)}) copy-start(bf16[768,768]{1,0:T(8,128)(2,1)} %param.11) | copy-start | bytes 3538948
  9.3 7.0 %copy-start.4 = (s32[1,1,2,128]{3,2,1,0:T(2,128)S(1)}, s32[1,1,2,128]{3,2,1,0:T(2,128)}, u32[]{:S(2)}) copy-start(s32[1,1,2,128]{3,2,1,0:T(2,128)} %param.13) | copy-start | bytes 3076
  11.9 5.6 %copy-start.5 = (s32[1,2,2]{2,1,0:T(2,128)S(1)}, s32[1,2,2]{2,1,0:T(2,128)}, u32[]{:S(2)}) copy-start(s32[1,2,2]{2,1,0:T(2,128)} %param.15) | copy-start | bytes 52
  11.9 5.8 %copy-start.6 = (f32[1,1,2,128]{3,2,1,0:T(2,128)S(1)}, f32[1,1,2,128]{3,2,1,0:T(2,128)}, u32[]{:S(2)}) copy-start(f32[1,1,2,128]{3,2,1,0:T(2,128)} %param.14) | copy-start | bytes 3076
  11.9 11.6 %all-to-all-start.1 = ((bf16[2,128,768]{2,1,0:T(8,128)(2,1)}), bf16[2,128,768]{2,1,0:T(8,128)(2,1)S(1)}, u32[]{:S(2)}, u32[]{:S(2)}) async-start(bf16[2,128,768]{2,1,0:T(8,128)(2,1)} %bitcast.9), calls=%async_computation.1 | async-start | bytes 786432 | tf_op jit(solution)/shard_map/all_to_all | solution.py:50
  16.3 166.8 %all-reduce.2.cloned.1.call-start = ((), (), s32[]{:S(2)}) async-start(), calls=%async_computation.4 | async-start | bytes 4718592 | tf_op jit(solution)/shard_map/psum | solution.py:90
  23.6 2.6 %copy-start.3 = (bf16[1,256,384]{2,1,0:T(8,128)(2,1)S(1)}, bf16[1,256,384]{2,1,0:T(8,128)(2,1)}, u32[]{:S(2)}) copy-start(bf16[1,256,384]{2,1,0:T(8,128)(2,1)} %param.9) | copy-start | bytes 589828
  25.6 160.8 %all-gather.2.cloned.1.call-start = ((), (), s32[]{:S(2)}) async-start(), calls=%async_computation.3 | async-start | bytes 6266880 | tf_op jit(solution)/shard_map/all_gather | solution.py:82
  29.5 9.0 %all-to-all-start = ((bf16[2,2,24576]{2,1,0:T(2,128)(2,1)}), bf16[2,2,24576]{2,1,0:T(2,128)(2,1)S(1)}, u32[]{:S(2)}, u32[]{:S(2)}) async-start(bf16[2,2,24576]{2,1,0:T(2,128)(2,1)} %reshape.152), calls=%async_computation | async-start | bytes 393216 | tf_op jit(solution)/shard_map/all_to_all | solution.py:46
  38.6 11.3 %all-to-all-start.2 = ((bf16[2,128,768]{2,1,0:T(8,128)(2,1)}), bf16[2,128,768]{2,1,0:T(8,128)(2,1)}, u32[]{:S(2)}, u32[]{:S(2)}) async-start(bf16[2,128,768]{2,1,0:T(8,128)(2,1)} %bitcast.13), calls=%async_computation.2 | async-start | bytes 786432 | tf_op jit(solution)/shard_map/all_to_all | solution.py:67
  44.7 8.2 %copy-start.1 = (bf16[1,256,768]{2,1,0:T(8,128)(2,1)S(1)}, bf16[1,256,768]{2,1,0:T(8,128)(2,1)}, u32[]{:S(2)}) copy-start(bf16[1,256,768]{2,1,0:T(8,128)(2,1)} %param.8) | copy-start | bytes 1179652
  53.3 133.1 %collective-permute-start = (bf16[1,2,768]{2,1,0:T(2,128)(2,1)S(1)}, bf16[1,2,768]{2,1,0:T(2,128)(2,1)S(1)}, u32[]{:S(2)}, u32[]{:S(2)}) collective-permute-start(bf16[1,2,768]{2,1,0:T(2,128)(2,1)S(1)} %get-tuple-element.3), channel_id=1, source_target_pairs={{1,0},{3,2},{5,4},{7,6},{9,8},{11,10},{13,12},{15,14},{17,16},{19,... | collective-permute-start | bytes 9224 | tf_op jit(solution)/shard_map/ppermute | solution.py:16
  54.6 136.2 %collective-permute-start.1 = (bf16[1,2,768]{2,1,0:T(2,128)(2,1)S(1)}, bf16[1,2,768]{2,1,0:T(2,128)(2,1)S(1)}, u32[]{:S(2)}, u32[]{:S(2)}) collective-permute-start(bf16[1,2,768]{2,1,0:T(2,128)(2,1)S(1)} %get-tuple-element.2), channel_id=1, source_target_pairs={{0,1},{2,3},{4,5},{6,7},{8,9},{10,11},{12,13},{14,15},{16,17},{18,... | collective-permute-start | bytes 9224 | tf_op jit(solution)/shard_map/ppermute | solution.py:15
  186.4 3.9 %copy-start.2 = (bf16[5,768,768]{2,1,0:T(8,128)(2,1)S(1)}, bf16[5,768,768]{2,1,0:T(8,128)(2,1)}, u32[]{:S(2)}) copy-start(bf16[5,768,768]{2,1,0:T(8,128)(2,1)} %all-gather.2.cloned.1.call-done) | copy-start | bytes 17694724
Sparse Core Ops, SparseCore 0:
  25.7 157.3 all-reduce.1
Sparse Core Ops, SparseCore 1:
  28.3 64.0 all-gather.1
where the time goes:
time: 200 us
  waiting for transfers between devices  137 us (68%)
  starting transfers between devices  18 us (9%)
  between operations  15.7 us (8%)
  other arithmetic  13.1 us (7%)
  matrix products  9.85 us (5%)
  local copies, waits for them, and re-layouts  6.27 us (3%)
    psum x1, waiting for transfers between devices, per_device(): pair_sum = lax.psum(pair_part, ('dp', 'seq'))  124 us
    dot_general x5, matrix products, per_device(): lax.dot_general(window, piece[tap], (((1,), (1,)), ((), ())), preferred_e...  6.13 us
    all_to_all x1, waiting for transfers between devices, per_device(): lax.all_to_all(outgoing, 'seq', split_axis=0, concat_axis=0, tiled=True)  5.81 us
    scatter-add x2, other arithmetic, per_device(): act_grad = pooled.at[accept_index].add(accept_term).at[send_index].add(re...  5.57 us
    ppermute x1, starting transfers between devices, with_halo(): before = lax.ppermute(last, axis, up)  4.72 us
    all_to_all x1, starting transfers between devices, per_device(): lax.all_to_all(outgoing, 'seq', split_axis=0, concat_axis=0, tiled=True)  4.34 us
    all_to_all x1, waiting for transfers between devices, per_device(): lax.all_to_all(trunk_grad, 'seq', split_axis=1, concat_axis=2, tiled=True)  4.32 us
    all_to_all x1, starting transfers between devices, per_device(): lax.all_to_all(donor_term.reshape(seq_count, slot_count, channels), 'seq'...  4.17 us
  transfers between devices with their start and end apart: 7, of which 4 were waited for; matrix products, arithmetic and copies ran while one was open for 11% of the time, Pallas kernels for 0%

commit v1 on v0

--- a/solution.py
+++ b/solution.py
@@ -87,7 +87,8 @@
             window, piece[tap], (((1,), (1,)), ((), ())), preferred_element_type=jnp.float32
         )
     input_grad = total.astype(jnp.bfloat16)
-    pair_sum = lax.psum(pair_part, ("dp", "seq"))
+    middle = lax.psum(pair_part, "seq")
+    pair_sum = lax.psum(middle, "dp")
     scale = 1.0 / math.sqrt(lax.axis_size("dp") * seq_count * seq_count * slot_count)
     return (input_grad[None], pair_sum * scale)
 

time: 200 us -> 272 us (1.36)
  waiting for transfers between devices: 137 us -> 210 us
    all_gather x1, waiting for transfers between devices: 0.01 us -> 58.1 us  [per_device(): piece = lax.all_gather(conv_weight, 'dp', axis=1, tiled=True)]
    psum x1 -> x2, waiting for transfers between devices: 124 us -> 141 us  [the longest x1 71.4 us: per_device(): pair_sum = lax.psum(middle, 'dp')]
  transfers between devices with their start and end apart: 7 -> 8, of which waited for: 4 -> 6; matrix products, arithmetic and copies ran while one was open for 11% -> 8% of each run, Pallas kernels for 0% -> 0%
where the time goes in v1:
time: 272 us; the launch traced here: 271 us
  waiting for transfers between devices  210 us (77%)
  starting transfers between devices  17.9 us (7%)
  between operations  14 us (5%)
  other arithmetic  13.1 us (5%)
  matrix products  9.85 us (4%)
  local copies, waits for them, and re-layouts  6.26 us (2%)
    psum x1, waiting for transfers between devices, per_device(): pair_sum = lax.psum(middle, 'dp')  71.4 us
    psum x1, waiting for transfers between devices, per_device(): middle = lax.psum(pair_part, 'seq')  69.3 us
    all_gather x1, waiting for transfers between devices, per_device(): piece = lax.all_gather(conv_weight, 'dp', axis=1, tiled=True)  58.1 us
    dot_general x5, matrix products, per_device(): lax.dot_general(window, piece[tap], (((1,), (1,)), ((), ())), preferred_e...  6.12 us
    all_to_all x1, waiting for transfers between devices, per_device(): lax.all_to_all(outgoing, 'seq', split_axis=0, concat_axis=0, tiled=True)  5.81 us
    scatter-add x2, other arithmetic, per_device(): act_grad = pooled.at[accept_index].add(accept_term).at[send_index].add(re...  5.57 us
  transfers between devices with their start and end apart: 8, of which 6 were waited for; matrix products, arithmetic and copies ran while one was open for 8% of the time, Pallas kernels for 0%

profile of v1, /device:TPU:0, one launch (start us, length us, event | category | flops | bytes accessed | tf_op | source)
XLA Modules:
  0.0 271.5 jit_solution(3508258621242941812)
XLA Ops:
  7.2 0.0 copy-start
  7.2 1.3 fusion.6
  8.5 0.0 copy-start.4
  8.5 0.7 compare_select_fusion
  9.2 1.9 gather_fusion
  11.1 0.0 copy-start.5
  11.1 0.0 copy-start.6
  11.1 4.3 %all-to-all-start.1 = ((bf16[2,128,768]{2,1,0:T(8,128)(2,1)}), bf16[2,128,768]{2,1,0:T(8,128)(2,1)S(1)}, u32[]{:S(2)}, u32[]{:S(2)}) async-start(bf16[2,128,768]{2,1,0:T(8,128)(2,1)} %bitcast.9), calls=%async_computation.1 | async-start | bytes 786432 | tf_op jit(solution)/shard_map/all_to_all | solution.py:50
  15.4 0.0 all-reduce.3.cloned.1.call-start
  15.4 0.0 copy-done.4
  15.5 1.2 gather_fusion.1
  16.7 0.0 copy-done.5
  16.7 0.2 dynamic-slice_reduce_fusion
  16.8 0.0 copy-done.6
  16.9 0.1 bitcast_select_fusion
  16.9 5.8 %all-to-all-done.1 = bf16[2,128,768]{2,1,0:T(8,128)(2,1)S(1)} async-done(((bf16[2,128,768]{2,1,0:T(8,128)(2,1)}), bf16[2,128,768]{2,1,0:T(8,128)(2,1)S(1)}, u32[]{:S(2)}, u32[]{:S(2)}) %all-to-all-start.1) | async-done | bytes 393248 | tf_op jit(solution)/shard_map/all_to_all | solution.py:50
  22.7 2.0 fusion.26
  24.7 0.0 copy-start.3
  24.7 0.0 all-reduce.3.cloned.1.call-update
  24.7 0.0 all-reduce.5.cloned.1.call-start
  24.8 69.3 %all-reduce.3.cloned.1.call-done = f32[768,768]{1,0:T(8,128)} async-done(((f32[768,768]{1,0:T(8,128)}), f32[768,768]{1,0:T(8,128)}) %all-reduce.3.cloned.1.call-update) | async-done | bytes 2359312 | tf_op jit(solution)/shard_map/psum | solution.py:90
  94.1 0.0 all-reduce.5.cloned.1.call-update
  94.1 0.0 all-gather.2.cloned.1.call-start
  94.2 0.7 all-gather.2.cloned.1.call-update
  94.9 0.0 copy-done.3
  94.9 0.3 copy.19
  95.2 0.5 broadcast.65
  95.7 1.8 reduce.2
  97.5 0.7 reshape.152
  98.2 3.4 %all-to-all-start = ((bf16[2,2,24576]{2,1,0:T(2,128)(2,1)}), bf16[2,2,24576]{2,1,0:T(2,128)(2,1)S(1)}, u32[]{:S(2)}, u32[]{:S(2)}) async-start(bf16[2,2,24576]{2,1,0:T(2,128)(2,1)} %reshape.152), calls=%async_computation | async-start | bytes 393216 | tf_op jit(solution)/shard_map/all_to_all | solution.py:46
  101.7 0.0 copy-done
  101.7 1.3 convolution_convert_fusion
  103.0 3.5 %all-to-all-done = bf16[2,2,24576]{2,1,0:T(2,128)(2,1)S(1)} async-done(((bf16[2,2,24576]{2,1,0:T(2,128)(2,1)}), bf16[2,2,24576]{2,1,0:T(2,128)(2,1)S(1)}, u32[]{:S(2)}, u32[]{:S(2)}) %all-to-all-start) | async-done | bytes 196640 | tf_op jit(solution)/shard_map/all_to_all | solution.py:46
  106.5 4.2 %all-to-all-start.2 = ((bf16[2,128,768]{2,1,0:T(8,128)(2,1)}), bf16[2,128,768]{2,1,0:T(8,128)(2,1)}, u32[]{:S(2)}, u32[]{:S(2)}) async-start(bf16[2,128,768]{2,1,0:T(8,128)(2,1)} %bitcast.13), calls=%async_computation.2 | async-start | bytes 786432 | tf_op jit(solution)/shard_map/all_to_all | solution.py:67
  110.7 0.2 reshape.153
  111.0 0.2 copy.15
  111.1 0.2 copy.16
  111.3 0.3 broadcast_in_dim.10
  111.6 0.5 reshape.111
  112.1 0.5 convolution_multiply_fusion
  112.6 0.0 copy-start.1
  112.6 2.5 scatter_fusion
  115.2 1.5 all-to-all-done.2
  116.6 3.0 %scatter_custom_fusion.1 = f32[256,768]{1,0:T(8,128)S(1)} fusion(f32[256,768]{1,0:T(8,128)S(1)} %scatter_fusion, s32[256]{0:T(256)S(1)} %bitcast.79, bf16[256,768]{1,0:T(8,128)(2,1)} %bitcast.27), kind=kCustom, calls=%fused_computation.33 | custom fusion | flops 393216 | bytes 1179648 | tf_op jit(solution)/shard_map/scatter-add | solution.py:78
  119.7 0.0 copy-done.1
  119.7 0.4 fusion.11
  120.1 1.3 collective-permute-start
  121.4 4.5 %collective-permute-start.1 = (bf16[1,2,768]{2,1,0:T(2,128)(2,1)S(1)}, bf16[1,2,768]{2,1,0:T(2,128)(2,1)S(1)}, u32[]{:S(2)}, u32[]{:S(2)}) collective-permute-start(bf16[1,2,768]{2,1,0:T(2,128)(2,1)S(1)} %get-tuple-element.2), channel_id=1, source_target_pairs={{0,1},{2,3},{4,5},{6,7},{8,9},{10,11},{12,13},{14,15},{16,17},{18,... | collective-permute-start | bytes 9224 | tf_op jit(solution)/shard_map/ppermute | solution.py:15
  125.9 71.4 %all-reduce.5.cloned.1.call-done = f32[768,768]{1,0:T(8,128)} async-done(((f32[768,768]{1,0:T(8,128)}), f32[768,768]{1,0:T(8,128)}) %all-reduce.5.cloned.1.call-update) | async-done | bytes 2359312 | tf_op jit(solution)/shard_map/psum | solution.py:91
  197.4 3.3 %broadcast_multiply_fusion = f32[768,768]{1,0:T(8,128)} fusion(f32[768,768]{1,0:T(8,128)} %all-reduce.5.cloned.1.call-done), kind=kLoop, calls=%fused_computation.23 | loop fusion | flops 589824 | bytes 4718592 | tf_op jit(solution)/shard_map/mul | solution.py:93
  200.6 0.0 collective-permute-done
  200.6 58.1 %all-gather.2.cloned.1.call-done = bf16[5,768,768]{2,1,0:T(8,128)(2,1)} async-done(((bf16[5,48,768]{2,1,0:T(8,128)(2,1)}), bf16[5,768,768]{2,1,0:T(8,128)(2,1)}) %all-gather.2.cloned.1.call-update) | async-done | bytes 5898256 | tf_op jit(solution)/shard_map/all_gather | solution.py:82
  258.8 0.0 copy-start.2
  258.8 1.9 fusion.2
  260.7 1.9 convolution_add_fusion.3
  262.6 0.0 copy-done.2
  262.6 0.5 convolution_add_fusion.2
  263.1 0.0 collective-permute-done.1
  263.1 0.5 convolution_add_fusion.1
  263.7 1.3 fusion.1
  (5 shorter events, 0.1 us)
Async XLA Ops:
  7.2 94.5 %copy-start = (bf16[768,768]{1,0:T(8,128)(2,1)S(1)}, bf16[768,768]{1,0:T(8,128)(2,1)}, u32[]{:S(2)}) copy-start(bf16[768,768]{1,0:T(8,128)(2,1)} %param.11) | copy-start | bytes 3538948
  8.5 7.0 %copy-start.4 = (s32[1,1,2,128]{3,2,1,0:T(2,128)S(1)}, s32[1,1,2,128]{3,2,1,0:T(2,128)}, u32[]{:S(2)}) copy-start(s32[1,1,2,128]{3,2,1,0:T(2,128)} %param.13) | copy-start | bytes 3076
  11.1 5.6 %copy-start.5 = (s32[1,2,2]{2,1,0:T(2,128)S(1)}, s32[1,2,2]{2,1,0:T(2,128)}, u32[]{:S(2)}) copy-start(s32[1,2,2]{2,1,0:T(2,128)} %param.15) | copy-start | bytes 52
  11.1 5.8 %copy-start.6 = (f32[1,1,2,128]{3,2,1,0:T(2,128)S(1)}, f32[1,1,2,128]{3,2,1,0:T(2,128)}, u32[]{:S(2)}) copy-start(f32[1,1,2,128]{3,2,1,0:T(2,128)} %param.14) | copy-start | bytes 3076
  11.1 11.6 %all-to-all-start.1 = ((bf16[2,128,768]{2,1,0:T(8,128)(2,1)}), bf16[2,128,768]{2,1,0:T(8,128)(2,1)S(1)}, u32[]{:S(2)}, u32[]{:S(2)}) async-start(bf16[2,128,768]{2,1,0:T(8,128)(2,1)} %bitcast.9), calls=%async_computation.1 | async-start | bytes 786432 | tf_op jit(solution)/shard_map/all_to_all | solution.py:50
  15.4 78.7 %all-reduce.3.cloned.1.call-start = ((), (), s32[]{:S(2)}) async-start(), calls=%async_computation.4 | async-start | bytes 4718592 | tf_op jit(solution)/shard_map/psum | solution.py:90
  24.7 70.2 %copy-start.3 = (bf16[1,256,384]{2,1,0:T(8,128)(2,1)S(1)}, bf16[1,256,384]{2,1,0:T(8,128)(2,1)}, u32[]{:S(2)}) copy-start(bf16[1,256,384]{2,1,0:T(8,128)(2,1)} %param.9) | copy-start | bytes 589828
  24.7 172.6 %all-reduce.5.cloned.1.call-start = ((), (), s32[]{:S(2)}) async-start(), calls=%async_computation.5 | async-start | bytes 4718592 | tf_op jit(solution)/shard_map/psum | solution.py:91
  94.1 164.6 %all-gather.2.cloned.1.call-start = ((), (), s32[]{:S(2)}) async-start(), calls=%async_computation.3 | async-start | bytes 6266880 | tf_op jit(solution)/shard_map/all_gather | solution.py:82
  98.2 8.2 %all-to-all-start = ((bf16[2,2,24576]{2,1,0:T(2,128)(2,1)}), bf16[2,2,24576]{2,1,0:T(2,128)(2,1)S(1)}, u32[]{:S(2)}, u32[]{:S(2)}) async-start(bf16[2,2,24576]{2,1,0:T(2,128)(2,1)} %reshape.152), calls=%async_computation | async-start | bytes 393216 | tf_op jit(solution)/shard_map/all_to_all | solution.py:46
  106.5 10.1 %all-to-all-start.2 = ((bf16[2,128,768]{2,1,0:T(8,128)(2,1)}), bf16[2,128,768]{2,1,0:T(8,128)(2,1)}, u32[]{:S(2)}, u32[]{:S(2)}) async-start(bf16[2,128,768]{2,1,0:T(8,128)(2,1)} %bitcast.13), calls=%async_computation.2 | async-start | bytes 786432 | tf_op jit(solution)/shard_map/all_to_all | solution.py:67
  112.6 7.1 %copy-start.1 = (bf16[1,256,768]{2,1,0:T(8,128)(2,1)S(1)}, bf16[1,256,768]{2,1,0:T(8,128)(2,1)}, u32[]{:S(2)}) copy-start(bf16[1,256,768]{2,1,0:T(8,128)(2,1)} %param.8) | copy-start | bytes 1179652
  120.1 80.6 %collective-permute-start = (bf16[1,2,768]{2,1,0:T(2,128)(2,1)S(1)}, bf16[1,2,768]{2,1,0:T(2,128)(2,1)S(1)}, u32[]{:S(2)}, u32[]{:S(2)}) collective-permute-start(bf16[1,2,768]{2,1,0:T(2,128)(2,1)S(1)} %get-tuple-element.3), channel_id=1, source_target_pairs={{1,0},{3,2},{5,4},{7,6},{9,8},{11,10},{13,12},{15,14},{17,16},{19,... | collective-permute-start | bytes 9224 | tf_op jit(solution)/shard_map/ppermute | solution.py:16
  121.4 141.8 %collective-permute-start.1 = (bf16[1,2,768]{2,1,0:T(2,128)(2,1)S(1)}, bf16[1,2,768]{2,1,0:T(2,128)(2,1)S(1)}, u32[]{:S(2)}, u32[]{:S(2)}) collective-permute-start(bf16[1,2,768]{2,1,0:T(2,128)(2,1)S(1)} %get-tuple-element.2), channel_id=1, source_target_pairs={{0,1},{2,3},{4,5},{6,7},{8,9},{10,11},{12,13},{14,15},{16,17},{18,... | collective-permute-start | bytes 9224 | tf_op jit(solution)/shard_map/ppermute | solution.py:15
  258.8 3.9 %copy-start.2 = (bf16[5,768,768]{2,1,0:T(8,128)(2,1)S(1)}, bf16[5,768,768]{2,1,0:T(8,128)(2,1)}, u32[]{:S(2)}) copy-start(bf16[5,768,768]{2,1,0:T(8,128)(2,1)} %all-gather.2.cloned.1.call-done) | copy-start | bytes 17694724
Sparse Core Ops, SparseCore 0:
  24.9 69.1 all-reduce.2
  98.1 99.2 all-reduce.4
  199.9 58.7 all-gather.1
